TPU v7x, 32 devices: a whole 2x2x4 slice. The times are simulated.
32 devices in a mesh: space: 8 (over y, x, core), vec: 4 (over z).
Axes of the slice: x: 2, y: 2, z: 4, core: 2. Of those that a mesh axis runs over, the one named last changes fastest.
Arguments:
- vectors: float32 [2, 3, 384, 8, 2048], P(None, None, 'vec', 'space'), may hold values from -0.375 to 0.375
- links: float32 [3, 2, 3, 3, 8, 2048], P(None, None, None, None, 'space'), may hold values from -3.5 to 3.5
- momenta: int32 [2, 3], replicated, may hold values from -2 to 2
- directions: int32 [3], replicated, may hold values from 0 to 2, each once
Outputs:
- elementals: float32 [2, 3, 2, 384, 384], P(None, None, None, 'space', 'vec')
Inputs may be any that keep to these rules, and one draw needn't show every extreme that they name: directions holds each of 0, 1, 2 once.
All inputs are finite; a program needn't handle non-finite values.
Results may differ from a plain program's by a relative error of at most 0.000098.
Values sent between devices are 32-bit elements; how exact they have to be, the bound alone decides.
No kernel may reach another device: no remote copies, remote signals or barrier semaphores. Data moves between devices by JAX's collectives and lax.ppermute only.
A program may use at most 128 MiB of HBM per device.

v0:
```python
import jax
import jax.numpy as jnp
from jax import lax
from jax.sharding import PartitionSpec as P

LY = 32
LZ = 64


def padded_2(shard, sides, width):
    for axis, dim in sides:
        size, length = (lax.axis_size(axis), shard.shape[dim])
        up = [(i, (i + 1) % size) for i in range(size)]
        down = [(j, i) for i, j in up]
        last = lax.slice_in_dim(shard, length - width, length, axis=dim)
        first = lax.slice_in_dim(shard, 0, width, axis=dim)
        before = lax.ppermute(last, axis, up)
        after = lax.ppermute(first, axis, down)
        shard = jnp.concatenate([before, shard, after], axis=dim)
    return shard


def shifted(value, axis, steps):
    count = lax.axis_size(axis)
    pairs = [(source, (source + steps) % count) for source in range(count)]
    return lax.ppermute(value, axis, pairs)


def site_shift(field, mu, step, plane_y, plane_z):
    shape = field.shape
    cube = field.reshape(shape[:-1] + (plane_y, plane_z))
    cube = jnp.roll(cube, -step, axis=-3 + mu)
    return cube.reshape(shape)


def color_apply(link, field, dagger):
    link_re = link[0]
    link_im = link[1]
    if dagger:
        link_re = jnp.swapaxes(link_re, 0, 1)
        link_im = -jnp.swapaxes(link_im, 0, 1)
    link_re = link_re[:, :, None]
    link_im = link_im[:, :, None]
    field_re = field[0][None]
    field_im = field[1][None]
    out_re = jnp.sum(link_re * field_re - link_im * field_im, axis=1)
    out_im = jnp.sum(link_re * field_im + link_im * field_re, axis=1)
    return jnp.stack([out_re, out_im], 0)


def phase_tables(momenta, xcoord, sites, extent_x, plane_y, plane_z):
    ycoord = sites // plane_z
    zcoord = sites % plane_z
    p0 = momenta[:, 0][:, None, None]
    p1 = momenta[:, 1][:, None, None]
    p2 = momenta[:, 2][:, None, None]
    frac = (p0 * xcoord % extent_x).astype(jnp.float32) / extent_x
    frac = frac + (p1 * ycoord[None, None] % plane_y).astype(jnp.float32) / plane_y
    frac = frac + (p2 * zcoord[None, None] % plane_z).astype(jnp.float32) / plane_z
    theta = 2.0 * jnp.pi * frac
    return (jnp.cos(theta), jnp.sin(theta))


def elemental_block(left_vecs, right_disp, cosine, sine):
    vec_re = left_vecs[0][None]
    vec_im = left_vecs[1][None]
    cosine = cosine[:, None, None]
    sine = sine[:, None, None]
    left_re = vec_re * cosine - vec_im * sine
    left_im = -(vec_re * sine + vec_im * cosine)
    left = jnp.stack([left_re, left_im], 1)
    gram = jnp.einsum(
        "mpcaxs,dqcbxs->mpadqb",
        left,
        right_disp,
        precision=lax.Precision.HIGHEST,
        preferred_element_type=jnp.float32,
    )
    part_re = gram[:, 0, :, :, 0] - gram[:, 1, :, :, 1]
    part_im = gram[:, 0, :, :, 1] + gram[:, 1, :, :, 0]
    stacked = jnp.stack([part_re, part_im], 1)
    return jnp.transpose(stacked, (0, 3, 1, 2, 4))


def on_device(vectors, links, momenta, directions):
    plane_y = LY
    plane_z = LZ
    extent_x = lax.axis_size("space")
    xcoord = lax.axis_index("space")
    padded = padded_2(vectors, (("space", 3),), 1)
    lower = shifted(links[0], "space", 1)
    forward_x = color_apply(links[0], padded[:, :, :, 2:3], False)
    backward_x = color_apply(lower, padded[:, :, :, 0:1], True)
    displaced_list = [forward_x - backward_x]
    for mu in (1, 2):
        forward = color_apply(links[mu], site_shift(vectors, mu, 1, plane_y, plane_z), False)
        backward = site_shift(color_apply(links[mu], vectors, True), mu, -1, plane_y, plane_z)
        displaced_list.append(forward - backward)
    displaced = jnp.stack(displaced_list, 0)
    site_count = vectors.shape[4]
    sites = jnp.arange(site_count, dtype=jnp.int32)
    cosine, sine = phase_tables(momenta, xcoord, sites, extent_x, plane_y, plane_z)
    block = elemental_block(
        lax.all_gather(vectors, "vec", axis=2, tiled=True), displaced, cosine, sine
    )
    reduced = lax.psum_scatter(block, "space", scatter_dimension=3, tiled=True)
    return jnp.take(reduced, directions, axis=1)


def solution(mesh):
    placed = (
        P(None, None, "vec", "space", None),
        P(None, None, None, None, "space", None),
        P(),
        P(),
    )
    return jax.shard_map(
        on_device,
        mesh=mesh,
        in_specs=placed,
        out_specs=P(None, None, None, "space", "vec"),
        check_vma=False,
    )
```

profile of v0, /device:TPU:0, one launch (start us, length us, event | category | flops | bytes accessed | tf_op | source)
XLA Modules:
  0.0 521.4 jit_solution(13569363760980879944)
XLA Ops:
  11.4 12.0 %copy.49 = f32[2,3,96,1,2048]{2,4,1,0,3:T(8,128)} copy(f32[2,3,96,1,2048]{4,3,2,1,0:T(1,128)} %param.4) | data formatting | bytes 9437184 | tf_op args[0]
  23.4 7.3 %slice.189 = f32[2,3,96,1,31,64]{2,5,4,1,0,3:T(8,128)} slice(f32[2,3,96,1,32,64]{2,5,4,1,0,3:T(8,128)} %bitcast.133), slice={[0:2], [0:3], [0:96], [0:1], [1:32], [0:64]} | slice | bytes 9142272 | tf_op jit(solution)/shard_map/jit(_roll_static)/slice | solution.py:32
  30.8 3.9 slice.193
  36.2 3.6 fusion.41
  42.0 11.1 %subtract_reduce_fusion.2 = (f32[3,96,2048]{2,1,0:T(8,128)}, f32[3,96,2048]{2,1,0:T(8,128)}, f32[3,96,2048]{2,1,0:T(8,128)}, f32[3,96,2048]{2,1,0:T(8,128)}) fusion(f32[3,96,2048]{2,1,0:T(8,128)S(1)} %get-tuple-element.50, f32[3,3,2048]{2,1,0:T(4,128)S(1)} %get-tuple-element.60, f32[3,96,2048]{2,1,0:T(8,128)S(1)} %get-tuple-element.51, ...), kind=kLoop, calls=%fused_computation.19 | loop fusion | flops 25952256 | bytes 14450688 | tf_op jit(solution)/shard_map/reduce_sum | solution.py:46
  55.4 3.6 copy.55
  59.0 6.9 %fusion.10 = (f32[1,3,96,1,32,64]{2,5,4,1,0,3:T(8,128)}, f32[1,3,96,1,32,64]{2,5,4,1,0,3:T(8,128)}) fusion(f32[2,3,96,1,31,64]{2,5,4,1,0,3:T(8,128)} %slice.189, f32[2,3,96,1,1,64]{2,5,4,1,0,3:T(8,128)S(1)} %slice.190), kind=kLoop, calls=%fused_computation.40 | loop fusion | flops 1179648 | bytes 9437184 | tf_op jit(solution)/shard_map/jit(_roll_static)/concatenate | solution.py:32
  76.2 3.5 copy.62
  79.7 7.0 %fusion.9 = (f32[1,3,96,1,32,64]{2,5,4,1,0,3:T(8,128)}, f32[1,3,96,1,32,64]{2,5,4,1,0,3:T(8,128)}) fusion(f32[2,3,96,1,32,63]{2,5,4,1,0,3:T(8,128)} %slice.193, f32[2,3,96,1,32,1]{2,5,4,1,0,3:T(1,128)S(1)} %slice.194), kind=kLoop, calls=%fused_computation.39 | loop fusion | flops 1179648 | bytes 9437184 | tf_op jit(solution)/shard_map/jit(_roll_static)/concatenate | solution.py:32
  93.7 5.2 %fusion.8 = f32[2,3,96,1,32,64]{2,5,4,1,3,0:T(8,128)} fusion(f32[1,3,96,1,32,64]{2,5,4,1,3,0:T(8,128)} %bitcast.142, f32[1,3,96,1,32,64]{2,5,4,1,3,0:T(8,128)S(1)} %bitcast.141), kind=kLoop, calls=%fused_computation.30 | loop fusion | flops 3538944 | bytes 9437184 | tf_op jit(solution)/shard_map/jit(_roll_static)/concatenate | solution.py:32
  99.8 3.7 fusion.7
  104.3 3.9 subtract_reduce_fusion.3
  108.3 4.7 subtract_reduce_fusion.1
  113.0 6.2 %copy.56 = f32[1,2,3,96,1,2048]{5,3,2,1,0,4:T(8,128)} copy(f32[1,2,3,96,1,2048]{3,5,2,1,4,0:T(8,128)} %bitcast.139) | data formatting | bytes 9437184 | tf_op jit(solution)/shard_map/reshape | solution.py:33
  119.2 6.6 %copy.63 = f32[1,2,3,96,1,2048]{5,3,2,1,0,4:T(8,128)} copy(f32[1,2,3,96,1,2048]{3,5,2,1,4,0:T(8,128)} %bitcast.140) | data formatting | bytes 9437184 | tf_op jit(solution)/shard_map/reshape | solution.py:33
  125.8 6.5 %maximum_subtract_fusion.1 = f32[1,2,3,96,1,2048]{5,3,2,1,0,4:T(8,128)} fusion(f32[1,2,3,96,1,2048]{5,3,2,1,0,4:T(8,128)} %copy.56, f32[1,1,3,96,1,2048]{5,3,2,1,0,4:T(8,128)} %bitcast.152, f32[1,1,3,96,1,2048]{5,3,2,1,0,4:T(8,128)S(1)} %bitcast.151), kind=kLoop, calls=%fused_computation.37 | loop fusion | flops 2359296 | bytes 14155776 | tf_op jit(solution)/shard_map/sub | solution.py:98
  137.4 6.4 %fusion.40 = (f32[1,3,96,1,2048]{4,3,2,1,0:T(1,128)S(1)}, f32[1,3,96,1,2048]{4,3,2,1,0:T(1,128)S(1)}) fusion(f32[2,3,96,1,2048]{4,3,2,1,0:T(1,128)} %collective-permute-done), kind=kLoop, calls=%fused_computation.124 | loop fusion | bytes 9437184 | tf_op jit(solution)/shard_map/slice | solution.py:44
  148.9 6.4 %fusion.39 = (f32[1,3,96,1,2048]{4,3,2,1,0:T(1,128)S(1)}, f32[1,3,96,1,2048]{4,3,2,1,0:T(1,128)S(1)}) fusion(f32[2,3,96,1,2048]{4,3,2,1,0:T(1,128)} %collective-permute-done.2), kind=kLoop, calls=%fused_computation.123 | loop fusion | bytes 9437184 | tf_op jit(solution)/shard_map/slice | solution.py:44
  163.2 170.9 %all-gather.2.cloned.1.call-done = f32[2,3,384,1,2048]{4,3,2,1,0:T(1,128)} async-done(((f32[2,3,96,1,2048]{4,3,2,1,0:T(1,128)}), f32[2,3,384,1,2048]{4,3,2,1,0:T(1,128)}) %all-gather.2.cloned.1.call-update) | async-done | bytes 18874384 | tf_op jit(solution)/shard_map/all_gather | solution.py:104
  334.1 13.3 %fusion.38 = (f32[1,3,384,1,2048]{4,3,2,1,0:T(1,128)}, f32[1,3,384,1,2048]{4,3,2,1,0:T(1,128)}) fusion(f32[2,3,384,1,2048]{4,3,2,1,0:T(1,128)} %all-gather.2.cloned.1.call-done), kind=kLoop, calls=%fused_computation.122 | loop fusion | bytes 37748736 | tf_op jit(solution)/shard_map/slice | solution.py:65
  347.3 13.7 %copy_bitcast_fusion = (f32[3,384,2048]{2,1,0:T(8,128)S(1)}, f32[3,384,2048]{2,1,0:T(8,128)S(1)}) fusion(f32[1,3,384,1,2048]{4,3,2,1,0:T(1,128)} %get-tuple-element.25, f32[1,3,384,1,2048]{4,3,2,1,0:T(1,128)} %get-tuple-element.24), kind=kLoop, calls=%fused_computation.12 | loop fusion | bytes 37748736
  361.0 13.2 %multiply_subtract_fusion = (f32[2,1,3,384,1,2048]{5,3,2,1,0,4:T(8,128)}, f32[2,1,3,384,1,2048]{5,3,2,1,0,4:T(8,128)}) fusion(f32[2,2048]{1,0:T(2,128)S(1)} %get-tuple-element.49, f32[3,384,2048]{2,1,0:T(8,128)S(1)} %get-tuple-element.70, f32[2,2048]{1,0:T(2,128)S(1)} %get-tuple-element.48, f32[3,384,2048]{2,1,0:T(8,128)S(1)} %get-tuple-element.71), kind=kLoop, calls=%fused_computation.6 | loop fusion | flops 33030144 | bytes 56655872 | tf_op jit(solution)/shard_map/sub | solution.py:69
  374.2 71.7 %fusion.11 = f32[2,2,384,3,2,96]{2,5,4,3,1,0:T(8,128)S(1)} fusion(f32[1,2,3,96,1,2048]{5,3,2,1,0,4:T(8,128)} %maximum_subtract_fusion.2, f32[1,2,3,96,1,2048]{5,3,2,1,0,4:T(8,128)} %maximum_subtract_fusion.1, f32[1,2,3,96,1,2048]{5,3,2,1,0,4:T(8,128)} %maximum_subtract_fusion, f32[2,1,3,384,1,2048]{5,3,2,1,0,4:T(8,128)} %get-tuple-element.23, ...), kind=kOutput, calls=%fused_computation.49 | convolution fusion | flops 65246330880 | bytes 55443456 | tf_op jit(solution)/shard_map/mpcaxs,dqcbxs->mpadqb/dot_general | solution.py:72
  450.7 60.5 %all-reduce.3.cloned.1.call-done = f32[2,3,2,384,96]{4,2,1,0,3:T(2,128)} async-done(((f32[2,3,2,384,96]{4,2,1,0,3:T(2,128)}), f32[2,3,2,384,96]{4,2,1,0,3:T(2,128)}) %all-reduce.3.cloned.1.call-update) | async-done | bytes 1769488
  (93 shorter events, 54.6 us)
Async XLA Ops:
  6.5 4.2 copy-start.10
  6.5 327.5 %all-gather.2.cloned.1.call-start = ((), (), s32[]{:S(2)}) async-start(), calls=%async_computation | async-start | bytes 23592960 | tf_op jit(solution)/shard_map/all_gather | solution.py:104
  7.3 504.0 %all-reduce.3.cloned.1.call-start = ((), (), s32[]{:S(2)}) async-start(), calls=%async_computation.1 | async-start | bytes 4718592
  7.3 130.1 %collective-permute-start = (f32[2,3,96,1,2048]{4,3,2,1,0:T(1,128)}, f32[2,3,96,1,2048]{4,3,2,1,0:T(1,128)}, u32[]{:S(2)}, u32[]{:S(2)}) collective-permute-start(f32[2,3,96,1,2048]{4,3,2,1,0:T(1,128)} %param.4), channel_id=1, source_target_pairs={{4,0},{8,4},{12,8},{16,12},{20,16},{24,20},{28,24},{0,28},{5,1},{9... | collective-permute-start | bytes 14155784 | tf_op jit(solution)/shard_map/ppermute | solution.py:18
  10.7 138.1 %collective-permute-start.2 = (f32[2,3,96,1,2048]{4,3,2,1,0:T(1,128)}, f32[2,3,96,1,2048]{4,3,2,1,0:T(1,128)}, u32[]{:S(2)}, u32[]{:S(2)}) collective-permute-start(f32[2,3,96,1,2048]{4,3,2,1,0:T(1,128)} %param.4), channel_id=1, source_target_pairs={{0,4},{4,8},{8,12},{12,16},{16,20},{20,24},{24,28},{28,0},{1,5},{5... | collective-permute-start | bytes 14155784 | tf_op jit(solution)/shard_map/ppermute | solution.py:17
  11.4 124.9 %collective-permute-start.1 = (f32[2,3,3,1,2048]{4,3,2,1,0:T(1,128)}, f32[2,3,3,1,2048]{4,3,2,1,0:T(1,128)}, u32[]{:S(2)}, u32[]{:S(2)}) collective-permute-start(f32[2,3,3,1,2048]{4,3,2,1,0:T(1,128)} %slice_bitcast_fusion.2), channel_id=1, source_target_pairs={{0,4},{4,8},{8,12},{12,16},{16,20},{20,24},{24,28},{28,0},{1,5},{5... | collective-permute-start | bytes 442376 | tf_op jit(solution)/shard_map/ppermute | solution.py:26
  23.4 7.3 %copy-start = (f32[2,3,96,1,2048]{2,4,1,0,3:T(8,128)S(1)}, f32[2,3,96,1,2048]{2,4,1,0,3:T(8,128)}, u32[]{:S(2)}) copy-start(f32[2,3,96,1,2048]{2,4,1,0,3:T(8,128)} %copy.49) | copy-start | bytes 14155780
  30.8 5.4 %slice-start = ((s8[4718592]{0:T(1024)(128)(4,1)}), s8[4194304]{0:T(1024)(128)(4,1)S(1)}, s32[]{:S(2)}) async-start(s8[4718592]{0:T(1024)(128)(4,1)} %bitcast.137), calls=%async_computation.2 | async-start | bytes 8388608
  30.8 5.4 %slice-start.1 = ((s8[4718592]{0:T(1024)(128)(4,1)}), s8[524288]{0:T(1024)(128)(4,1)S(1)}, s32[]{:S(2)}) async-start(s8[4718592]{0:T(1024)(128)(4,1)} %bitcast.137), calls=%async_computation.3 | async-start | bytes 1048576
  86.7 6.8 %copy-start.16 = (s32[2,3]{1,0:T(2,128)S(1)}, s32[2,3]{1,0:T(2,128)}, u32[]{:S(2)}) copy-start(s32[2,3]{1,0:T(2,128)} %param.6) | copy-start | bytes 76
  93.7 5.3 %copy-start.14 = (f32[1,1,3,3,1,2048]{5,4,3,2,1,0:T(1,128)S(1)}, f32[1,1,3,3,1,2048]{5,4,3,2,1,0:T(1,128)}, u32[]{:S(2)}) copy-start(f32[1,1,3,3,1,2048]{5,4,3,2,1,0:T(1,128)} %get-tuple-element.41) | copy-start | bytes 221188
  93.7 5.3 %copy-start.15 = (f32[1,1,3,3,1,2048]{5,4,3,2,1,0:T(1,128)S(1)}, f32[1,1,3,3,1,2048]{5,4,3,2,1,0:T(1,128)}, u32[]{:S(2)}) copy-start(f32[1,1,3,3,1,2048]{5,4,3,2,1,0:T(1,128)} %get-tuple-element.42) | copy-start | bytes 221188
  93.7 5.4 %copy-start.12 = (f32[1,1,3,3,1,2048]{5,4,3,2,1,0:T(1,128)S(1)}, f32[1,1,3,3,1,2048]{5,4,3,2,1,0:T(1,128)}, u32[]{:S(2)}) copy-start(f32[1,1,3,3,1,2048]{5,4,3,2,1,0:T(1,128)} %get-tuple-element.44) | copy-start | bytes 221188
  93.7 5.4 %copy-start.13 = (f32[1,1,3,3,1,2048]{5,4,3,2,1,0:T(1,128)S(1)}, f32[1,1,3,3,1,2048]{5,4,3,2,1,0:T(1,128)}, u32[]{:S(2)}) copy-start(f32[1,1,3,3,1,2048]{5,4,3,2,1,0:T(1,128)} %get-tuple-element.45) | copy-start | bytes 221188
  93.7 5.5 %copy-start.2 = (f32[3,96,2048]{1,2,0:T(8,128)S(1)}, f32[3,96,2048]{1,2,0:T(8,128)}, u32[]{:S(2)}) copy-start(f32[3,96,2048]{1,2,0:T(8,128)} %copy.61) | copy-start | bytes 7077892
  93.7 6.0 %copy-start.3 = (f32[3,96,2048]{1,2,0:T(8,128)S(1)}, f32[3,96,2048]{1,2,0:T(8,128)}, u32[]{:S(2)}) copy-start(f32[3,96,2048]{1,2,0:T(8,128)} %copy.62) | copy-start | bytes 7077892
  99.8 3.8 copy-start.6
  99.8 4.6 copy-start.7
  104.3 3.9 copy-start.8
  104.3 3.9 copy-start.9
  125.8 6.6 %copy-start.1 = (f32[1,2,3,96,1,2048]{5,3,2,1,0,4:T(8,128)S(1)}, f32[1,2,3,96,1,2048]{5,3,2,1,0,4:T(8,128)}, u32[]{:S(2)}) copy-start(f32[1,2,3,96,1,2048]{5,3,2,1,0,4:T(8,128)} %copy.63) | copy-start | bytes 14155780
  125.8 6.6 %copy-start.4 = (f32[3,96,2048]{2,1,0:T(8,128)S(1)}, f32[3,96,2048]{2,1,0:T(8,128)}, u32[]{:S(2)}) copy-start(f32[3,96,2048]{2,1,0:T(8,128)} %get-tuple-element.13) | copy-start | bytes 7077892
  125.8 7.1 %copy-start.5 = (f32[3,96,2048]{2,1,0:T(8,128)S(1)}, f32[3,96,2048]{2,1,0:T(8,128)}, u32[]{:S(2)}) copy-start(f32[3,96,2048]{2,1,0:T(8,128)} %get-tuple-element.14) | copy-start | bytes 7077892
  446.1 4.6 copy-start.17
  (2 other events, 7.1 us)
Sparse Core Ops, SparseCore 0:
  8.9 325.1 all-gather.1
  449.6 61.6 all-reduce.2
where the time goes:
time: 531 us; the launch traced here: 521 us
  waiting for transfers between devices  232 us (44%)
  local copies, waits for them, and re-layouts  122 us (23%)
  other arithmetic  77.1 us (15%)
  matrix products  71.7 us (14%)
  between operations  14.8 us (3%)
    all_gather x1, waiting for transfers between devices, on_device(): lax.all_gather(vectors, 'vec', axis=2, tiled=True)  171 us
    dot_general x1, matrix products, elemental_block(): jnp.einsum('mpcaxs,dqcbxs->mpadqb', left, right_disp, precision=lax.Preci...  71.7 us
    unnamed x3, waiting for transfers between devices  61.3 us
    unnamed x52, local copies, waits for them, and re-layouts  36.2 us
    reduce_sum x5, other arithmetic, color_apply(): out_re = jnp.sum(link_re * field_re - link_im * field_im, axis=1)  25.2 us
    concatenate x4, other arithmetic, site_shift(): cube = jnp.roll(cube, -step, axis=-3 + mu)  22.9 us
    slice x3, local copies, waits for them, and re-layouts, color_apply(): field_re = field[0][None]  16.5 us
    mul x7, local copies, waits for them, and re-layouts, color_apply(): out_re = jnp.sum(link_re * field_re - link_im * field_im, axis=1)  13.8 us
  transfers between devices with their start and end apart: 5, of which 2 were waited for; matrix products, arithmetic and copies ran while one was open for 29% of the time, Pallas kernels for 0%

commit v1 on v0

--- a/solution.py
+++ b/solution.py
@@ -5,6 +5,27 @@
 
 LY = 32
 LZ = 64
+
+
+def collect(x, axis, dim):
+    devices, index, extent = (lax.axis_size(axis), lax.axis_index(axis), x.shape[dim])
+    forward = [(i, (i + 1) % devices) for i in range(devices)]
+    left = [(i, (i - 1) % devices) for i in range(devices)]
+    result = jnp.zeros((*x.shape[:dim], devices * extent, *x.shape[dim + 1 :]), x.dtype)
+    result = lax.dynamic_update_slice_in_dim(result, x, index * extent, axis=dim)
+    from_left = from_right = x
+    middle = devices // 2
+    for step in range(1, middle + 1):
+        from_left = lax.ppermute(from_left, axis, forward)
+        result = lax.dynamic_update_slice_in_dim(
+            result, from_left, (index - step) % devices * extent, axis=dim
+        )
+        if step < devices - middle:
+            from_right = lax.ppermute(from_right, axis, left)
+            result = lax.dynamic_update_slice_in_dim(
+                result, from_right, (index + step) % devices * extent, axis=dim
+            )
+    return result
 
 
 def padded_2(shard, sides, width):
@@ -100,9 +121,7 @@
     site_count = vectors.shape[4]
     sites = jnp.arange(site_count, dtype=jnp.int32)
     cosine, sine = phase_tables(momenta, xcoord, sites, extent_x, plane_y, plane_z)
-    block = elemental_block(
-        lax.all_gather(vectors, "vec", axis=2, tiled=True), displaced, cosine, sine
-    )
+    block = elemental_block(collect(vectors, "vec", 2), displaced, cosine, sine)
     reduced = lax.psum_scatter(block, "space", scatter_dimension=3, tiled=True)
     return jnp.take(reduced, directions, axis=1)
 

time: 531 us -> 493 us (0.928); the launches traced: 521 us -> 489 us
  waiting for transfers between devices: 232 us -> 184 us
  local copies, waits for them, and re-layouts: 122 us -> 138 us
    all_gather x1 -> x0, waiting for transfers between devices: 171 us -> none  [on_device(): lax.all_gather(vectors, 'vec', axis=2, tiled=True)]
    ppermute x0 -> x3, waiting for transfers between devices: none -> 123 us  [the longest x2 94.7 us: collect(): from_left = lax.ppermute(from_left, axis, forward)]
    dynamic_update_slice x0 -> x4, local copies, waits for them, and re-layouts: none -> 22.2 us  [the longest x2 11.1 us: collect(): lax.dynamic_update_slice_in_dim(result, from_left, (index - step) % devic...]
    slice x1 -> x0, local copies, waits for them, and re-layouts: 13.3 us -> none  [elemental_block(): vec_re = left_vecs[0][None]]
    unnamed x52 -> x55, local copies, waits for them, and re-layouts: 36.2 us -> 24.6 us
    broadcast_in_dim x0 -> x1, local copies, waits for them, and re-layouts: none -> 8.87 us  [collect(): jnp.zeros((*x.shape[:dim], devices * extent, *x.shape[dim + 1:]), x.dtype)]
    mul x0 -> x1, local copies, waits for them, and re-layouts: none -> 7.21 us  [elemental_block(): left_re = vec_re * cosine - vec_im * sine]
    concatenate x4, other arithmetic: 22.9 us -> 16 us  [site_shift(): cube = jnp.roll(cube, -step, axis=-3 + mu)]
  transfers between devices with their start and end apart: 5 -> 7, of which waited for: 2 -> 3; matrix products, arithmetic and copies ran while one was open for 29% -> 36% of each run, Pallas kernels for 0% -> 0%
where the time goes in v1:
time: 493 us; the launch traced here: 489 us
  waiting for transfers between devices  184 us (37%)
  local copies, waits for them, and re-layouts  138 us (28%)
  other arithmetic  72.5 us (15%)
  matrix products  71.7 us (15%)
  between operations  14.9 us (3%)
  starting transfers between devices  7.43 us (2%)
    ppermute x2, waiting for transfers between devices, collect(): from_left = lax.ppermute(from_left, axis, forward)  94.7 us
    dot_general x1, matrix products, elemental_block(): jnp.einsum('mpcaxs,dqcbxs->mpadqb', left, right_disp, precision=lax.Preci...  71.7 us
    unnamed x2, waiting for transfers between devices  61.2 us
    ppermute x1, waiting for transfers between devices, collect(): from_right = lax.ppermute(from_right, axis, left)  28.3 us
    reduce_sum x5, other arithmetic, color_apply(): out_re = jnp.sum(link_re * field_re - link_im * field_im, axis=1)  26.3 us
    unnamed x55, local copies, waits for them, and re-layouts  24.6 us
    slice x3, local copies, waits for them, and re-layouts, color_apply(): field_re = field[0][None]  21 us
    concatenate x4, other arithmetic, site_shift(): cube = jnp.roll(cube, -step, axis=-3 + mu)  16 us
  transfers between devices with their start and end apart: 7, of which 3 were waited for; matrix products, arithmetic and copies ran while one was open for 36% of the time, Pallas kernels for 0%

profile of v1, /device:TPU:0, one launch (start us, length us, event | category | flops | bytes accessed | tf_op | source)
XLA Modules:
  0.0 488.8 jit_solution(3058985636810327286)
XLA Ops:
  17.2 8.2 %fusion.40 = (f32[1,3,96,1,2048]{4,3,2,1,0:T(1,128)S(1)}, f32[1,3,96,1,2048]{4,3,2,1,0:T(1,128)}) fusion(f32[2,3,96,1,2048]{4,3,2,1,0:T(1,128)} %param.4), kind=kLoop, calls=%fused_computation.128 | loop fusion | bytes 9437184 | tf_op jit(solution)/shard_map/slice | solution.py:65
  25.4 11.9 %copy.65 = f32[2,3,96,1,2048]{2,4,1,0,3:T(8,128)} copy(f32[2,3,96,1,2048]{4,3,2,1,0:T(1,128)} %param.4) | data formatting | bytes 9437184 | tf_op args[0]
  37.3 6.5 %slice.189 = f32[2,3,96,1,31,64]{2,5,4,1,0,3:T(8,128)} slice(f32[2,3,96,1,32,64]{2,5,4,1,0,3:T(8,128)} %bitcast.133), slice={[0:2], [0:3], [0:96], [0:1], [1:32], [0:64]} | slice | bytes 9142272 | tf_op jit(solution)/shard_map/jit(_roll_static)/slice | solution.py:53
  51.6 10.3 %subtract_reduce_fusion.2 = (f32[3,96,2048]{2,1,0:T(8,128)}, f32[3,96,2048]{2,1,0:T(8,128)}, f32[3,96,2048]{2,1,0:T(8,128)}, f32[3,96,2048]{2,1,0:T(8,128)S(1)}) fusion(f32[3,96,2048]{2,1,0:T(8,128)S(1)} %get-tuple-element.50, f32[3,3,2048]{2,1,0:T(4,128)S(1)} %get-tuple-element.60, f32[3,96,2048]{2,1,0:T(8,128)S(1)} %get-tuple-element.51, ...), kind=kLoop, calls=%fused_computation.19 | loop fusion | flops 25952256 | bytes 14450688 | tf_op jit(solution)/shard_map/reduce_sum | solution.py:67
  74.9 5.4 %fusion.8 = f32[2,3,96,1,32,64]{2,5,4,1,3,0:T(8,128)} fusion(f32[1,3,96,1,32,64]{2,5,4,1,3,0:T(8,128)} %bitcast.152, f32[1,3,96,1,32,64]{2,5,4,1,3,0:T(8,128)} %bitcast.151), kind=kLoop, calls=%fused_computation.30 | loop fusion | flops 3538944 | bytes 9437184 | tf_op jit(solution)/shard_map/jit(_roll_static)/concatenate | solution.py:53
  80.4 3.9 fusion.10
  105.1 5.7 %subtract_reduce_fusion.3 = (f32[3,96,2048]{2,1,0:T(8,128)S(1)}, f32[3,96,2048]{2,1,0:T(8,128)}) fusion(f32[3,96,2048]{2,1,0:T(8,128)} %copy.67, f32[3,3,2048]{2,1,0:T(4,128)S(1)} %get-tuple-element.54, f32[3,96,2048]{2,1,0:T(8,128)} %copy.66, f32[3,3,2048]{2,1,0:T(4,128)S(1)} %get-tuple-element.55), kind=kLoop, calls=%fused_computation.21 | loop fusion | flops 12976128 | bytes 9584640 | tf_op jit(solution)/shard_map/reduce_sum | solution.py:67
  110.8 4.7 subtract_reduce_fusion.1
  115.5 8.9 %broadcast_in_dim.12 = f32[2,3,384,1,2048]{4,2,1,3,0:T(8,128)} broadcast(f32[]{:T(128)} %constant.109.clone.1), dimensions={} | broadcast | bytes 18874372 | tf_op jit(solution)/shard_map/broadcast_in_dim | solution.py:14
  124.3 4.4 copy_dynamic-update-slice_fusion.3
  128.7 6.3 %copy.72 = f32[1,2,3,96,1,2048]{5,3,2,1,0,4:T(8,128)} copy(f32[1,2,3,96,1,2048]{3,5,2,1,4,0:T(8,128)} %bitcast.141) | data formatting | bytes 9437184 | tf_op jit(solution)/shard_map/reshape | solution.py:54
  135.0 6.2 %copy.79 = f32[1,2,3,96,1,2048]{5,3,2,1,0,4:T(8,128)} copy(f32[1,2,3,96,1,2048]{3,5,2,1,4,0:T(8,128)} %bitcast.142) | data formatting | bytes 9437184 | tf_op jit(solution)/shard_map/reshape | solution.py:54
  141.2 6.5 %maximum_subtract_fusion.1 = f32[1,2,3,96,1,2048]{5,3,2,1,0,4:T(8,128)} fusion(f32[1,2,3,96,1,2048]{5,3,2,1,0,4:T(8,128)} %copy.72, f32[1,1,3,96,1,2048]{5,3,2,1,0,4:T(8,128)} %bitcast.156, f32[1,1,3,96,1,2048]{5,3,2,1,0,4:T(8,128)S(1)} %bitcast.155), kind=kLoop, calls=%fused_computation.37 | loop fusion | flops 2359296 | bytes 14155776 | tf_op jit(solution)/shard_map/sub | solution.py:119
  153.5 6.4 %fusion.39 = (f32[1,3,96,1,2048]{4,3,2,1,0:T(1,128)S(1)}, f32[1,3,96,1,2048]{4,3,2,1,0:T(1,128)S(1)}) fusion(f32[2,3,96,1,2048]{4,3,2,1,0:T(1,128)} %collective-permute-done.3), kind=kLoop, calls=%fused_computation.127 | loop fusion | bytes 9437184 | tf_op jit(solution)/shard_map/slice | solution.py:65
  164.9 6.4 %fusion.38 = (f32[1,3,96,1,2048]{4,3,2,1,0:T(1,128)S(1)}, f32[1,3,96,1,2048]{4,3,2,1,0:T(1,128)S(1)}) fusion(f32[2,3,96,1,2048]{4,3,2,1,0:T(1,128)} %collective-permute-done.5), kind=kLoop, calls=%fused_computation.126 | loop fusion | bytes 9437184 | tf_op jit(solution)/shard_map/slice | solution.py:65
  179.5 6.7 %copy_dynamic-update-slice_fusion.2 = f32[2,3,384,1,2048]{4,2,1,3,0:T(8,128)} fusion(f32[2,3,384,1,2048]{4,2,1,3,0:T(8,128)} %copy_dynamic-update-slice_fusion.3, s32[]{:T(128)S(6)} %select_n.99, f32[2,3,96,1,2048]{4,3,2,1,0:T(1,128)} %collective-permute-done), kind=kLoop, calls=%fused_computation.41 | loop fusion | bytes 9437188 | tf_op jit(solution)/shard_map/dynamic_update_slice | solution.py:20
  186.2 28.3 %collective-permute-done.1 = f32[2,3,96,1,2048]{4,3,2,1,0:T(1,128)} collective-permute-done((f32[2,3,96,1,2048]{4,3,2,1,0:T(1,128)}, f32[2,3,96,1,2048]{4,3,2,1,0:T(1,128)}, u32[]{:S(2)}, u32[]{:S(2)}) %collective-permute-start.1) | collective-permute-done | bytes 4718624 | tf_op jit(solution)/shard_map/ppermute | solution.py:24
  214.5 6.7 %copy_dynamic-update-slice_fusion.1 = f32[2,3,384,1,2048]{4,2,1,3,0:T(8,128)} fusion(f32[2,3,384,1,2048]{4,2,1,3,0:T(8,128)} %copy_dynamic-update-slice_fusion.2, s32[]{:T(128)S(6)} %select_n.101, f32[2,3,96,1,2048]{4,3,2,1,0:T(1,128)} %collective-permute-done.1), kind=kLoop, calls=%fused_computation.40 | loop fusion | bytes 9437188 | tf_op jit(solution)/shard_map/dynamic_update_slice | solution.py:25
  221.2 94.7 %collective-permute-done.2 = f32[2,3,96,1,2048]{4,3,2,1,0:T(1,128)S(1)} collective-permute-done((f32[2,3,96,1,2048]{4,3,2,1,0:T(1,128)}, f32[2,3,96,1,2048]{4,3,2,1,0:T(1,128)S(1)}, u32[]{:S(2)}, u32[]{:S(2)}) %collective-permute-start.2) | collective-permute-done | bytes 4718624 | tf_op jit(solution)/shard_map/ppermute | solution.py:19
  315.9 4.4 copy_dynamic-update-slice_fusion
  320.3 7.2 %slice_bitcast_fusion.1 = (f32[3,384,2048]{2,1,0:T(8,128)S(1)}, f32[3,384,2048]{2,1,0:T(8,128)S(1)}) fusion(f32[2,3,384,1,2048]{4,2,1,3,0:T(8,128)} %copy_dynamic-update-slice_fusion), kind=kLoop, calls=%fused_computation.13 | loop fusion | bytes 37748736 | tf_op jit(solution)/shard_map/mul | solution.py:90
  327.5 13.3 %multiply_subtract_fusion = (f32[2,1,3,384,1,2048]{5,3,2,1,0,4:T(8,128)}, f32[2,1,3,384,1,2048]{5,3,2,1,0,4:T(8,128)}) fusion(f32[2,2048]{1,0:T(2,128)S(1)} %get-tuple-element.49, f32[3,384,2048]{2,1,0:T(8,128)S(1)} %get-tuple-element.25, f32[2,2048]{1,0:T(2,128)S(1)} %get-tuple-element.48, f32[3,384,2048]{2,1,0:T(8,128)S(1)} %get-tuple-element.24), kind=kLoop, calls=%fused_computation.6 | loop fusion | flops 33030144 | bytes 56655872 | tf_op jit(solution)/shard_map/sub | solution.py:90
  340.8 71.7 %fusion.11 = f32[2,2,384,3,2,96]{2,5,4,3,1,0:T(8,128)S(1)} fusion(f32[1,2,3,96,1,2048]{5,3,2,1,0,4:T(8,128)} %maximum_subtract_fusion.2, f32[1,2,3,96,1,2048]{5,3,2,1,0,4:T(8,128)} %maximum_subtract_fusion.1, f32[1,2,3,96,1,2048]{5,3,2,1,0,4:T(8,128)} %maximum_subtract_fusion, f32[2,1,3,384,1,2048]{5,3,2,1,0,4:T(8,128)} %get-tuple-element.23, ...), kind=kOutput, calls=%fused_computation.53 | convolution fusion | flops 65246330880 | bytes 55443456 | tf_op jit(solution)/shard_map/mpcaxs,dqcbxs->mpadqb/dot_general | solution.py:93
  417.4 61.2 %all-reduce.3.cloned.1.call-done = f32[2,3,2,384,96]{4,2,1,0,3:T(2,128)} async-done(((f32[2,3,2,384,96]{4,2,1,0,3:T(2,128)}), f32[2,3,2,384,96]{4,2,1,0,3:T(2,128)}) %all-reduce.3.cloned.1.call-update) | async-done | bytes 1769488
  (106 shorter events, 78.1 us)
Async XLA Ops:
  6.5 472.0 %all-reduce.3.cloned.1.call-start = ((), (), s32[]{:S(2)}) async-start(), calls=%async_computation | async-start | bytes 4718592
  6.5 146.4 %collective-permute-start = (f32[2,3,96,1,2048]{4,3,2,1,0:T(1,128)}, f32[2,3,96,1,2048]{4,3,2,1,0:T(1,128)}, u32[]{:S(2)}, u32[]{:S(2)}) collective-permute-start(f32[2,3,96,1,2048]{4,3,2,1,0:T(1,128)} %param.4), channel_id=1, source_target_pairs={{0,1},{1,2},{2,3},{3,0},{4,5},{5,6},{6,7},{7,4},{8,9},{9,10},{10,1... | collective-permute-start | bytes 14155784 | tf_op jit(solution)/shard_map/ppermute | solution.py:19
  9.6 204.9 %collective-permute-start.1 = (f32[2,3,96,1,2048]{4,3,2,1,0:T(1,128)}, f32[2,3,96,1,2048]{4,3,2,1,0:T(1,128)}, u32[]{:S(2)}, u32[]{:S(2)}) collective-permute-start(f32[2,3,96,1,2048]{4,3,2,1,0:T(1,128)} %param.4), channel_id=1, source_target_pairs={{0,3},{1,0},{2,1},{3,2},{4,7},{5,4},{6,5},{7,6},{8,11},{9,8},{10,9... | collective-permute-start | bytes 14155784 | tf_op jit(solution)/shard_map/ppermute | solution.py:24
  11.6 141.9 %collective-permute-start.3 = (f32[2,3,96,1,2048]{4,3,2,1,0:T(1,128)}, f32[2,3,96,1,2048]{4,3,2,1,0:T(1,128)}, u32[]{:S(2)}, u32[]{:S(2)}) collective-permute-start(f32[2,3,96,1,2048]{4,3,2,1,0:T(1,128)} %param.4), channel_id=1, source_target_pairs={{4,0},{8,4},{12,8},{16,12},{20,16},{24,20},{28,24},{0,28},{5,1},{9... | collective-permute-start | bytes 14155784 | tf_op jit(solution)/shard_map/ppermute | solution.py:39
  13.2 151.7 %collective-permute-start.5 = (f32[2,3,96,1,2048]{4,3,2,1,0:T(1,128)}, f32[2,3,96,1,2048]{4,3,2,1,0:T(1,128)}, u32[]{:S(2)}, u32[]{:S(2)}) collective-permute-start(f32[2,3,96,1,2048]{4,3,2,1,0:T(1,128)} %param.4), channel_id=1, source_target_pairs={{0,4},{4,8},{8,12},{12,16},{16,20},{20,24},{24,28},{28,0},{1,5},{5... | collective-permute-start | bytes 14155784 | tf_op jit(solution)/shard_map/ppermute | solution.py:38
  14.8 137.1 %collective-permute-start.4 = (f32[2,3,3,1,2048]{4,3,2,1,0:T(1,128)}, f32[2,3,3,1,2048]{4,3,2,1,0:T(1,128)}, u32[]{:S(2)}, u32[]{:S(2)}) collective-permute-start(f32[2,3,3,1,2048]{4,3,2,1,0:T(1,128)} %slice_bitcast_fusion.4), channel_id=1, source_target_pairs={{0,4},{4,8},{8,12},{12,16},{16,20},{20,24},{24,28},{28,0},{1,5},{5... | collective-permute-start | bytes 442376 | tf_op jit(solution)/shard_map/ppermute | solution.py:47
  37.3 6.5 %copy-start = (f32[2,3,96,1,2048]{2,4,1,0,3:T(8,128)S(1)}, f32[2,3,96,1,2048]{2,4,1,0,3:T(8,128)}, u32[]{:S(2)}) copy-start(f32[2,3,96,1,2048]{2,4,1,0,3:T(8,128)} %copy.65) | copy-start | bytes 14155780
  68.8 5.9 %copy-start.14 = (s32[2,3]{1,0:T(2,128)S(1)}, s32[2,3]{1,0:T(2,128)}, u32[]{:S(2)}) copy-start(s32[2,3]{1,0:T(2,128)} %param.6) | copy-start | bytes 76
  71.1 9.2 %slice-start.4 = ((s8[6094848]{0:T(1024)(128)(4,1)}), s8[1900544]{0:T(1024)(128)(4,1)S(1)}, s32[]{:S(2)}) async-start(s8[6094848]{0:T(1024)(128)(4,1)} %bitcast.143), calls=%async_computation.5 | async-start | bytes 3801088
  74.9 5.5 %slice-start.5 = ((s8[6094848]{0:T(1024)(128)(4,1)}), s8[4194304]{0:T(1024)(128)(4,1)S(1)}, s32[]{:S(2)}) async-start(s8[6094848]{0:T(1024)(128)(4,1)} %bitcast.143), calls=%async_computation.6 | async-start | bytes 8388608
  80.4 5.1 %copy-start.5 = (f32[3,96,2048]{1,2,0:T(8,128)S(1)}, f32[3,96,2048]{1,2,0:T(8,128)}, u32[]{:S(2)}) copy-start(f32[3,96,2048]{1,2,0:T(8,128)} %copy.78) | copy-start | bytes 7077892
  80.4 9.1 %slice-start.2 = ((s8[6291456]{0:T(1024)(128)(4,1)}), s8[4194304]{0:T(1024)(128)(4,1)S(1)}, s32[]{:S(2)}) async-start(s8[6291456]{0:T(1024)(128)(4,1)} %bitcast.139), calls=%async_computation.3 | async-start | bytes 8388608
  85.5 4.0 slice-start.3
  105.1 5.7 %copy-start.8 = (f32[3,96,2048]{2,1,0:T(8,128)S(1)}, f32[3,96,2048]{2,1,0:T(8,128)}, u32[]{:S(2)}) copy-start(f32[3,96,2048]{2,1,0:T(8,128)} %copy.73) | copy-start | bytes 7077892
  105.1 5.7 %copy-start.9 = (f32[3,96,2048]{2,1,0:T(8,128)S(1)}, f32[3,96,2048]{2,1,0:T(8,128)}, u32[]{:S(2)}) copy-start(f32[3,96,2048]{2,1,0:T(8,128)} %copy.74) | copy-start | bytes 7077892
  105.1 5.7 %copy-start.10 = (f32[3,3,2048]{2,1,0:T(4,128)S(1)}, f32[3,3,2048]{2,1,0:T(4,128)}, u32[]{:S(2)}) copy-start(f32[3,3,2048]{2,1,0:T(4,128)} %get-tuple-element.52) | copy-start | bytes 221188
  105.1 5.7 %copy-start.11 = (f32[3,3,2048]{2,1,0:T(4,128)S(1)}, f32[3,3,2048]{2,1,0:T(4,128)}, u32[]{:S(2)}) copy-start(f32[3,3,2048]{2,1,0:T(4,128)} %get-tuple-element.53) | copy-start | bytes 221188
  110.8 13.6 %slice-start = ((s8[4718592]{0:T(1024)(128)(4,1)}), s8[4194304]{0:T(1024)(128)(4,1)S(1)}, s32[]{:S(2)}) async-start(s8[4718592]{0:T(1024)(128)(4,1)} %bitcast.137), calls=%async_computation.1 | async-start | bytes 8388608
  115.5 8.9 %slice-start.1 = ((s8[4718592]{0:T(1024)(128)(4,1)}), s8[524288]{0:T(1024)(128)(4,1)S(1)}, s32[]{:S(2)}) async-start(s8[4718592]{0:T(1024)(128)(4,1)} %bitcast.137), calls=%async_computation.2 | async-start | bytes 1048576
  141.2 6.5 %copy-start.1 = (f32[1,2,3,96,1,2048]{5,3,2,1,0,4:T(8,128)S(1)}, f32[1,2,3,96,1,2048]{5,3,2,1,0,4:T(8,128)}, u32[]{:S(2)}) copy-start(f32[1,2,3,96,1,2048]{5,3,2,1,0,4:T(8,128)} %copy.79) | copy-start | bytes 14155780
  141.2 6.5 %copy-start.6 = (f32[3,96,2048]{2,1,0:T(8,128)S(1)}, f32[3,96,2048]{2,1,0:T(8,128)}, u32[]{:S(2)}) copy-start(f32[3,96,2048]{2,1,0:T(8,128)} %get-tuple-element.13) | copy-start | bytes 7077892
  141.2 7.1 %copy-start.7 = (f32[3,96,2048]{2,1,0:T(8,128)S(1)}, f32[3,96,2048]{2,1,0:T(8,128)}, u32[]{:S(2)}) copy-start(f32[3,96,2048]{2,1,0:T(8,128)} %get-tuple-element.14) | copy-start | bytes 7077892
  153.0 162.9 %collective-permute-start.2 = (f32[2,3,96,1,2048]{4,3,2,1,0:T(1,128)}, f32[2,3,96,1,2048]{4,3,2,1,0:T(1,128)S(1)}, u32[]{:S(2)}, u32[]{:S(2)}) collective-permute-start(f32[2,3,96,1,2048]{4,3,2,1,0:T(1,128)} %collective-permute-done), channel_id=1, source_target_pairs={{0,1},{1,2},{2,3},{3,0},{4,5},{5,6},{6,7},{7,4},{8,9},{9,10},{10,1... | collective-permute-start | bytes 14155784 | tf_op jit(solution)/shard_map/ppermute | solution.py:19
  412.7 4.6 copy-start.15
  (6 other events, 21.7 us)
Sparse Core Ops, SparseCore 0:
  416.2 62.2 all-reduce.2
